TPU v7x, 32 devices: a whole 2x2x4 slice. The times are simulated.
32 devices in a mesh: dp: 4 (over y, core), item: 8 (over z, x).
Axes of the slice: x: 2, y: 2, z: 4, core: 2. Of those that a mesh axis runs over, the one named last changes fastest.
Arguments:
- query: bfloat16 [32, 256], P(('dp', 'item')), may hold values from -40 to 40
- item_table: bfloat16 [65536, 256], P(('dp', 'item')), may hold values from -2.5 to 2.5
- context_features: bfloat16 [32, 512], P(('dp', 'item')), may hold values from -6 to 6
- candidates: int32 [32, 1024], P(('dp', 'item')), may hold values from 0 to 65535, as said below
- lengths: int32 [32], P(('dp', 'item')), may hold values from 128 to 1024, as said below
- logged_slot: int32 [32], P(('dp', 'item')), may hold values from 0 to 1023, as said below
- logging_prop: int32 [32], P(('dp', 'item')), may hold values from 256 to 4095
- w_first: bfloat16 [768, 512], replicated, may hold values from -0.21875 to 0.21875
- w_second: bfloat16 [512, 512], replicated, may hold values from -0.25 to 0.25
- w_score: bfloat16 [512], replicated, may hold values from -0.5 to 0.5
Outputs:
- section_logp: float32 [32, 1024], P(('dp', 'item'))
- log_weight: float32 [32], P(('dp', 'item'))
Inputs may be any that keep to these rules, and one draw needn't show every extreme that they name: `candidates`: item ids. Among the 1024 candidate slots held by one device (its single context), at most 48 name items of any one block of 2048 consecutive ids, and for every device some block is named exactly 48 times. `lengths`: some context's list has 1024 live slots and some context's list has 128. `logged_slot`: below the context's length; the context with the longest list logs its last slot.
All inputs are finite; a program needn't handle non-finite values.
Results may differ from a plain program's by a relative error of at most 0.0003.
Values may be sent and summed in bfloat16 or wider, within the bound.
A program may use at most 64 MiB of HBM per device.

v0:
```python
import math

import jax
import jax.numpy as jnp
from jax import lax
from jax.sharding import PartitionSpec as P


def merged(array, axis, combine):
    everything = jax.tree.map(lambda part: lax.all_gather(part, axis), array)
    leading = jax.tree.map(lambda part: part[0], everything)

    def step(k, so_far):
        return combine(so_far, jax.tree.map(lambda part: part[k], everything))

    return lax.fori_loop(1, lax.axis_size(axis), step, leading)


def combine_pairs(earlier, later):
    new_max = jnp.maximum(earlier[0], later[0])
    new_sum = earlier[1] * jnp.exp(earlier[0] - new_max) + later[1] * jnp.exp(later[0] - new_max)
    return (new_max, new_sum)


def body(
    query,
    item_table,
    context_features,
    candidates,
    lengths,
    logged_slot,
    logging_prop,
    w_first,
    w_second,
    w_score,
):
    device_count = lax.axis_size("dp") * lax.axis_size("item")
    item_rows = item_table.shape[0]
    width = item_table.shape[1]
    own_count = query.shape[0]
    slot_count = candidates.shape[1]
    gathered = lax.all_gather(query, ("dp", "item"), axis=0, tiled=True)
    context_total = gathered.shape[0]
    block_rows = min(512, item_rows)
    slabs = item_table.reshape(item_rows // block_rows, block_rows, width)

    def sweep(running, slab_rows):
        running_max, running_sum = running
        logits = lax.dot_general(
            gathered, slab_rows, (((1,), (1,)), ((), ())), preferred_element_type=jnp.float32
        )
        new_max = jnp.maximum(running_max, jnp.max(logits, axis=1))
        new_sum = running_sum * jnp.exp(running_max - new_max) + jnp.sum(
            jnp.exp(logits - new_max[:, None]), axis=1
        )
        return ((new_max, new_sum), None)

    initial = (
        jnp.full((context_total,), -1e30, jnp.float32),
        jnp.zeros((context_total,), jnp.float32),
    )
    (local_max, local_sum), unused_out = lax.scan(sweep, initial, slabs)
    first_context = lax.axis_index(("dp", "item")) * own_count
    global_max, global_sum = merged((local_max, local_sum), ("dp", "item"), combine_pairs)
    log_norm = lax.dynamic_slice_in_dim(global_max + jnp.log(global_sum), first_context, own_count)
    capacity = max(2, 3 * own_count * slot_count // (2 * device_count))
    flat_ids = candidates.reshape(-1)
    holder = flat_ids // item_rows
    same_holder = holder[:, None] == holder[None, :]
    earlier_slot = jnp.arange(flat_ids.shape[0])[None, :] < jnp.arange(flat_ids.shape[0])[:, None]
    holder_rank = jnp.sum((same_holder & earlier_slot).astype(jnp.int32), axis=1)
    bucket = holder * capacity + holder_rank
    outgoing = jnp.full((device_count * capacity,), -1, jnp.int32).at[bucket].set(flat_ids)
    outgoing = outgoing.reshape(lax.axis_size("dp"), lax.axis_size("item"), capacity)
    first_item = lax.axis_index(("dp", "item")) * item_rows
    asked_ids = lax.all_to_all(
        lax.all_to_all(outgoing, "dp", split_axis=0, concat_axis=0, tiled=True),
        "item",
        split_axis=1,
        concat_axis=1,
        tiled=True,
    )
    local_index = jnp.clip(asked_ids - first_item, 0, item_rows - 1)
    fetched = lax.all_to_all(
        lax.all_to_all(item_table[local_index], "dp", split_axis=0, concat_axis=0, tiled=True),
        "item",
        split_axis=1,
        concat_axis=1,
        tiled=True,
    )
    cand_rows = fetched.reshape(device_count * capacity, width)[bucket]
    rows_by_context = cand_rows.reshape(own_count, slot_count, width)
    gen_logit = jnp.einsum("cd,ckd->ck", query, rows_by_context, preferred_element_type=jnp.float32)
    feature_width = context_features.shape[1]
    context_part = jnp.dot(
        context_features, w_first[:feature_width], preferred_element_type=jnp.float32
    )
    item_part = jnp.dot(cand_rows, w_first[feature_width:], preferred_element_type=jnp.float32)
    item_part = item_part.reshape(own_count, slot_count, -1)
    hidden = jax.nn.silu(item_part + context_part[:, None, :]).astype(jnp.bfloat16)
    hidden = hidden.reshape(own_count * slot_count, -1)
    second = jax.nn.silu(jnp.dot(hidden, w_second, preferred_element_type=jnp.float32)).astype(
        jnp.bfloat16
    )
    score = jnp.dot(second, w_score, preferred_element_type=jnp.float32).reshape(
        own_count, slot_count
    )
    positions = jnp.arange(slot_count, dtype=jnp.int32)
    live_slots = positions[None, :] < lengths[:, None]
    masked = jnp.where(live_slots, score, jnp.float32(-1e30))
    rank_peak = jnp.max(masked, axis=1)
    rank_norm = rank_peak + jnp.log(
        jnp.sum(
            jnp.where(live_slots, jnp.exp(masked - rank_peak[:, None]), jnp.float32(0.0)), axis=1
        )
    )
    total_items = item_rows * device_count
    section = jnp.where(
        live_slots,
        score - rank_norm[:, None] + gen_logit - log_norm[:, None] + math.log(total_items),
        jnp.float32(0.0),
    )
    chosen = jnp.sum(
        jnp.where(positions[None, :] == logged_slot[:, None], section, jnp.float32(0.0)), axis=1
    )
    log_weight = (
        chosen
        + jnp.log(lengths.astype(jnp.float32))
        - jnp.log(logging_prop.astype(jnp.float32) / 1024.0)
    )
    return (section, log_weight)


def solution(mesh):
    in_specs = (
        P(("dp", "item"), None),
        P(("dp", "item"), None),
        P(("dp", "item"), None),
        P(("dp", "item"), None),
        P(("dp", "item")),
        P(("dp", "item")),
        P(("dp", "item")),
        P(),
        P(),
        P(),
    )
    out_specs = (P(("dp", "item"), None), P(("dp", "item")))
    return jax.shard_map(body, mesh=mesh, in_specs=in_specs, out_specs=out_specs, check_vma=False)
```

profile of v0, /device:TPU:0, one launch (start us, length us, event | category | flops | bytes accessed | tf_op | source)
XLA Modules:
  0.0 184.3 jit_solution(8159638173040724396)
XLA Ops:
  0.6 0.0 copy-start
  0.6 0.8 and_select_fusion
  1.4 0.7 add_select_fusion
  2.1 0.5 convert_reduce_fusion
  2.6 0.7 compare_select_fusion.1
  3.4 4.5 %scatter_custom_fusion = s32[1536]{0:T(1024)S(1)} fusion(s32[1024]{0:T(1024)S(1)} %bitcast.83, s32[1024]{0:T(1024)} %bitcast.81, s32[]{:T(128)} %constant.87.clone.1), kind=kCustom, calls=%fused_computation.53 | custom fusion | bytes 6656 | tf_op jit(solution)/shard_map/scatter | solution.py:73
  7.8 0.1 reshape.181
  7.9 0.1 reshape.234
  8.0 7.9 %all_to_all.20 = s32[4,1,384]{2,1,0:T(1,128)S(1)} all-to-all(s32[4,1,384]{2,1,0:T(1,128)S(1)} %reshape.234), channel_id=1, replica_groups=mesh['dp'=4,'item'=8] {'dp'}, dimensions={0} | all-to-all | bytes 12288 | tf_op jit(solution)/shard_map/all_to_all | solution.py:77
  15.9 0.5 broadcast.187
  16.4 0.7 reduce.8
  17.1 0.1 reshape.235
  17.2 0.7 reshape.236
  17.8 5.8 %all-to-all-start.1 = ((s32[8,1,192]{2,1,0:T(1,128)}), s32[8,1,192]{2,1,0:T(1,128)S(1)}, u32[]{:S(2)}, u32[]{:S(2)}) async-start(s32[8,1,192]{2,1,0:T(1,128)} %reshape.236), calls=%async_computation.1 | async-start | bytes 16384 | tf_op jit(solution)/shard_map/all_to_all | solution.py:76
  23.7 66.8 %all-gather.2 = bf16[32,1,256]{2,1,0:T(2,128)(2,1)S(1)} all-gather(bf16[1,1,256]{2,1,0:T(2,128)(2,1)} %bitcast.85), channel_id=1, replica_groups=mesh['dp'=4,'item'=8] {'dp','item'}, dimensions={0}, use_global_device_ids=true | all-gather | bytes 16896 | tf_op jit(solution)/shard_map/all_gather | solution.py:42
  90.5 0.7 reduce.9
  91.1 0.1 reshape.237
  91.2 0.1 reshape.188
  91.3 5.9 %gather_fusion = bf16[1536,256]{1,0:T(8,128)(2,1)} fusion(bf16[2048,256]{1,0:T(8,128)(2,1)} %param.15, s32[2048]{0:T(1024)S(1)} %pad_clamp_fusion), kind=kCustom, calls=%fused_computation | custom fusion | bytes 1579008 | tf_op jit(solution)/shard_map/gather | solution.py:85
  97.2 3.5 %all-to-all-start.2 = ((bf16[4,8,48,256]{3,2,1,0:T(8,128)(2,1)}), bf16[4,8,48,256]{3,2,1,0:T(8,128)(2,1)S(1)}, u32[]{:S(2)}, u32[]{:S(2)}) async-start(bf16[4,8,48,256]{3,2,1,0:T(8,128)(2,1)} %bitcast.8), calls=%async_computation.2 | async-start | bytes 1572864 | tf_op jit(solution)/shard_map/all_to_all | solution.py:85
  100.7 6.0 %while.31 = (s32[]{:T(128)}, f32[32]{0:T(128)S(1)}, f32[32]{0:T(128)S(1)}, bf16[4,512,256]{2,1,0:T(8,128)(2,1)}, bf16[32,256]{1,0:T(8,128)(2,1)S(1)}, /*index=5*/s32[]{:T(128)}, s32[]{:T(128)}) while((s32[]{:T(128)}, f32[32]{0:T(128)S(1)}, f32[32]{0:T(128)S(1)}, bf16[4,512,256]{2,1,0:T(8,128)(2,1)}, bf16[32,256]{1,0:T(8,128)(2,1)S(1)}, ...), condition=%wide.region_7.8_spmd.clone, body=%wide.region_4.7_spmd.clone.sunk | while | flops 8437923 | bytes 411864 | solution.py:62
  100.7 1.2 fusion.42
  102.0 0.2 exponential_reduce_fusion.2
  102.2 1.2 fusion.42
  103.5 0.2 exponential_reduce_fusion.2
  103.7 1.2 fusion.42
  105.0 0.2 exponential_reduce_fusion.2
  105.2 1.2 fusion.42
  106.5 0.2 exponential_reduce_fusion.2
  106.7 0.2 dynamic-update-slice
  106.9 0.2 dynamic-update-slice.1
  107.2 37.0 %all-reduce.2 = (f32[1024]{0:T(1024)S(1)}, f32[1024]{0:T(1024)S(1)}) all-reduce(f32[1024]{0:T(1024)S(1)} %dynamic-update-slice, f32[1024]{0:T(1024)S(1)} %dynamic-update-slice.1), channel_id=2, replica_groups=mesh['dp'=4,'item'=8] {'dp','item'}, use_global_device_ids=true, to_apply=%add | all-reduce | flops 2048 | bytes 16384
  144.1 0.1 reshape.210
  144.2 0.1 reshape.211
  144.3 1.0 copy.24
  145.2 6.1 %all-to-all-start.3 = ((bf16[4,8,48,256]{3,2,0,1:T(8,128)(2,1)}), bf16[4,8,48,256]{3,2,0,1:T(8,128)(2,1)S(1)}, u32[]{:S(2)}, u32[]{:S(2)}) async-start(bf16[4,8,48,256]{3,2,0,1:T(8,128)(2,1)} %copy.24), calls=%async_computation.3 | async-start | bytes 1572864 | tf_op jit(solution)/shard_map/all_to_all | solution.py:84
  151.3 1.4 while.30
  154.8 0.7 dynamic_slice.27
  155.4 0.2 fusion.13
  155.6 15.6 %all-to-all-done.3 = bf16[4,8,48,256]{3,2,0,1:T(8,128)(2,1)S(1)} async-done(((bf16[4,8,48,256]{3,2,0,1:T(8,128)(2,1)}), bf16[4,8,48,256]{3,2,0,1:T(8,128)(2,1)S(1)}, u32[]{:S(2)}, u32[]{:S(2)}) %all-to-all-start.3) | async-done | bytes 786464 | tf_op jit(solution)/shard_map/all_to_all | solution.py:84
  171.2 0.1 copy.25
  171.3 3.9 %gather_fusion.1 = bf16[1024,256]{1,0:T(8,128)(2,1)S(1)} fusion(bf16[1536,256]{1,0:T(8,128)(2,1)S(1)} %bitcast.74, s32[1024]{0:T(1024)S(1)} %broadcast_clamp_fusion), kind=kCustom, calls=%fused_computation.1 | custom fusion | bytes 1052672 | tf_op jit(solution)/shard_map/gather | solution.py:91
  175.2 0.2 fusion.24
  175.5 1.4 multiply_convert_fusion
  176.9 0.4 fusion.28
  177.3 0.6 fusion.22
  177.9 1.3 select_reduce_fusion.1
  180.6 1.9 %select_reduce_fusion = (f32[]{:T(128)}, f32[1024]{0:T(1024)}) fusion(s32[]{:T(128)} %bitcast.72, f32[]{:T(128)} %bitcast.15, f32[1024]{0:T(1024)S(1)} %bitcast.82, f32[1024]{0:T(1024)S(1)} %bitcast.78, f32[]{:T(128)S(6)} %add.144, s32[]{:T(128)} %bitcast.71), kind=kLoop, calls=%fused_computation.48 | loop fusion | flops 9215 | bytes 12308 | tf_op jit(solution)/shard_map/reduce_sum | solution.py:123
  (68 shorter events, 1.0 us)
Async XLA Ops:
  0.6 174.8 %copy-start = (bf16[512,512]{1,0:T(8,128)(2,1)S(1)}, bf16[512,512]{1,0:T(8,128)(2,1)}, u32[]{:S(2)}) copy-start(bf16[512,512]{1,0:T(8,128)(2,1)} %param.22) | copy-start | bytes 1572868
  17.8 72.6 %all-to-all-start.1 = ((s32[8,1,192]{2,1,0:T(1,128)}), s32[8,1,192]{2,1,0:T(1,128)S(1)}, u32[]{:S(2)}, u32[]{:S(2)}) async-start(s32[8,1,192]{2,1,0:T(1,128)} %reshape.236), calls=%async_computation.1 | async-start | bytes 16384 | tf_op jit(solution)/shard_map/all_to_all | solution.py:76
  97.2 47.1 %all-to-all-start.2 = ((bf16[4,8,48,256]{3,2,1,0:T(8,128)(2,1)}), bf16[4,8,48,256]{3,2,1,0:T(8,128)(2,1)S(1)}, u32[]{:S(2)}, u32[]{:S(2)}) async-start(bf16[4,8,48,256]{3,2,1,0:T(8,128)(2,1)} %bitcast.8), calls=%async_computation.2 | async-start | bytes 1572864 | tf_op jit(solution)/shard_map/all_to_all | solution.py:85
  145.2 7.5 %copy-start.4 = (bf16[512]{0:T(512)(128)(2,1)S(1)}, bf16[512]{0:T(512)(128)(2,1)}, u32[]{:S(2)}) copy-start(bf16[512]{0:T(512)(128)(2,1)} %param.23) | copy-start | bytes 3076
  145.2 10.2 %copy-start.1 = (bf16[768,512]{1,0:T(8,128)(2,1)S(1)}, bf16[768,512]{1,0:T(8,128)(2,1)}, u32[]{:S(2)}) copy-start(bf16[768,512]{1,0:T(8,128)(2,1)} %param.21) | copy-start | bytes 2359300
  145.2 10.2 %copy-start.3 = (bf16[1,512]{1,0:T(2,128)(2,1)S(1)}, bf16[1,512]{1,0:T(2,128)(2,1)}, u32[]{:S(2)}) copy-start(bf16[1,512]{1,0:T(2,128)(2,1)} %param.16) | copy-start | bytes 3076
  145.2 25.9 %all-to-all-start.3 = ((bf16[4,8,48,256]{3,2,0,1:T(8,128)(2,1)}), bf16[4,8,48,256]{3,2,0,1:T(8,128)(2,1)S(1)}, u32[]{:S(2)}, u32[]{:S(2)}) async-start(bf16[4,8,48,256]{3,2,0,1:T(8,128)(2,1)} %copy.24), calls=%async_computation.3 | async-start | bytes 1572864 | tf_op jit(solution)/shard_map/all_to_all | solution.py:84
  171.2 4.0 %copy-start.2 = (bf16[1,256]{1,0:T(2,128)(2,1)S(1)}, bf16[1,256]{1,0:T(2,128)(2,1)}, u32[]{:S(2)}) copy-start(bf16[1,256]{1,0:T(2,128)(2,1)} %param.14) | copy-start | bytes 1540
where the time goes:
time: 185 us; the launch traced here: 184 us
  blocking collectives  112 us (61%)
  local copies, waits for them, and re-layouts  18.2 us (10%)
  waiting for transfers between devices  15.6 us (8%)
  starting transfers between devices  15.4 us (8%)
  other arithmetic  9.64 us (5%)
  matrix products  7.17 us (4%)
  between operations  6.05 us (3%)
    all_gather x1, blocking collectives, body(): gathered = lax.all_gather(query, ('dp', 'item'), axis=0, tiled=True)  66.8 us
    unnamed x1, blocking collectives  37 us
    all_to_all x1, waiting for transfers between devices, body(): lax.all_to_all(lax.all_to_all(item_table[local_index], 'dp', split_axis=0...  15.6 us
    all_to_all x1, blocking collectives, body(): lax.all_to_all(outgoing, 'dp', split_axis=0, concat_axis=0, tiled=True)  7.87 us
    all_to_all x1, starting transfers between devices, body(): lax.all_to_all(lax.all_to_all(item_table[local_index], 'dp', split_axis=0...  6.09 us
    gather x1, local copies, waits for them, and re-layouts, body(): item_table[local_index]  5.85 us
    all_to_all x1, starting transfers between devices, body(): lax.all_to_all(lax.all_to_all(outgoing, 'dp', split_axis=0, concat_axis=0...  5.81 us
    dot_general x4, matrix products, sweep(): lax.dot_general(gathered, slab_rows, (((1,), (1,)), ((), ())), preferred_...  4.97 us
  transfers between devices with their start and end apart: 3, of which 1 were waited for; matrix products, arithmetic and copies ran while one was open for 4% of the time, Pallas kernels for 0%

commit v1 on v0

v1 whole, which is shorter than its diff:
```python
import functools
import math

import jax
import jax.numpy as jnp
from jax import lax
from jax.experimental import pallas as pl
from jax.experimental.pallas import tpu as pltpu
from jax.sharding import PartitionSpec as P

F32 = jnp.float32
BF16 = jnp.bfloat16
LANES = 128
NT = (((1,), (1,)), ((), ()))
NN = (((1,), (0,)), ((), ()))
TN = (((0,), (0,)), ((), ()))


def round_up(value, step):
    return (value + step - 1) // step * step


def dot(left, right, dims):
    return lax.dot_general(left, right, dims, preferred_element_type=F32)


def silu(v):
    half = v * 0.5
    return half + half * jnp.tanh(half)


def kernel(
    dp_size,
    item_size,
    cap,
    query_ref,
    feature_ref,
    cand_ref,
    length_ref,
    slot_ref,
    prop_ref,
    table_hbm,
    first_hbm,
    second_hbm,
    score_ref,
    section_ref,
    weight_ref,
    table,
    first,
    second_w,
    send1,
    recv1,
    send2,
    recv2,
    load_sem,
    send_sem,
    recv_sem,
    own_sem,
):
    n = dp_size * item_size
    item_rows, width = table.shape
    slots = cand_ref.shape[1]
    feature_width = feature_ref.shape[1]
    hidden_width = first.shape[1]
    gen_at = round_up(cap, 8)
    max_at = 2 * gen_at
    me = lax.axis_index("dp") * item_size + lax.axis_index("item")

    loads = [
        pltpu.make_async_copy(first_hbm, first, load_sem.at[0]),
        pltpu.make_async_copy(table_hbm, table, load_sem.at[1]),
        pltpu.make_async_copy(second_hbm, second_w, load_sem.at[2]),
    ]
    for load in loads:
        load.start()

    def device(j):
        peer = lax.rem(me + j, n)
        return peer, {"dp": lax.div(peer, item_size), "item": lax.rem(peer, item_size)}

    barrier = pltpu.get_barrier_semaphore()

    @pl.loop(1, n)
    def greet(j):
        peer, where = device(j)
        pl.semaphore_signal(barrier, inc=1, device_id=where, device_id_type=pl.DeviceIdType.MESH)

    ids = cand_ref[...]
    holder = lax.div(ids, item_rows)
    local = ids - holder * item_rows
    high = lax.div(local, LANES).astype(F32)
    low = lax.rem(local, LANES).astype(F32)
    held = (lax.broadcasted_iota(jnp.int32, (n, slots), 0) == holder).astype(F32)
    blocks = slots // LANES
    stacked = jnp.concatenate(
        [held[:, b * LANES : (b + 1) * LANES] for b in range(blocks)], axis=0
    ).astype(BF16)
    before = (
        lax.broadcasted_iota(jnp.int32, (LANES, LANES), 0)
        < lax.broadcasted_iota(jnp.int32, (LANES, LANES), 1)
    ).astype(F32)
    counter = jnp.concatenate([before, jnp.ones((LANES, LANES), F32)], axis=1).astype(BF16)
    counts = dot(stacked, counter, NN)
    total = jnp.zeros((n, LANES), F32)
    rank_parts = []
    for b in range(blocks):
        here = counts[b * n : (b + 1) * n]
        place = here[:, :LANES] + total
        rank_parts.append(
            jnp.sum(held[:, b * LANES : (b + 1) * LANES] * place, axis=0, keepdims=True)
        )
        total = total + here[:, LANES:]
    rank = jnp.concatenate(rank_parts, axis=1)
    at_rank = (
        lax.broadcasted_iota(jnp.int32, (LANES, slots), 0).astype(F32) == rank
    ).astype(F32)
    parts = jnp.concatenate([held * high, held * low], axis=0).astype(BF16)
    asked = dot(parts, at_rank.astype(BF16), NT)
    asked = asked[:n] * float(LANES) + asked[n:]

    loads[0].wait()
    context_part = dot(feature_ref[...], first[:feature_width, :], NN)
    send1[:, 0, :width] = jnp.broadcast_to(query_ref[...].astype(F32), (n, width))
    send1[:, 0, width : width + hidden_width] = jnp.broadcast_to(context_part, (n, hidden_width))
    send1[:, 0, width + hidden_width :] = asked

    pl.semaphore_wait(barrier, n - 1)

    def exchange(source, target, index):
        @pl.loop(1, n)
        def send(j):
            peer, where = device(j)
            pltpu.make_async_remote_copy(
                src_ref=source.at[pl.ds(peer, 1)],
                dst_ref=target.at[pl.ds(me, 1)],
                send_sem=send_sem.at[index],
                recv_sem=recv_sem.at[index],
                device_id=where,
                device_id_type=pl.DeviceIdType.MESH,
            ).start()

        own = pltpu.make_async_copy(
            source.at[pl.ds(me, 1)], target.at[pl.ds(me, 1)], own_sem.at[index]
        )
        own.start()
        own.wait()

    def arrived(target, index):
        pltpu.make_async_copy(
            target.at[pl.ds(0, n - 1)], target.at[pl.ds(0, n - 1)], recv_sem.at[index]
        ).wait()

    def sent(source, index):
        pltpu.make_async_copy(
            source.at[pl.ds(0, n - 1)], source.at[pl.ds(0, n - 1)], send_sem.at[index]
        ).wait()

    exchange(send1, recv1, 0)
    loads[1].wait()
    loads[2].wait()
    arrived(recv1, 0)

    queries = recv1[:, 0, :width]
    logits = dot(queries.astype(BF16), table[...], NT)
    local_max = jnp.max(logits, axis=1, keepdims=True)
    local_sum = jnp.sum(jnp.exp(logits - local_max), axis=1, keepdims=True)

    lane = lax.broadcasted_iota(jnp.int32, (n, LANES), 1)
    result = jnp.where(lane == max_at, local_max, 0.0)
    result = jnp.where(lane == max_at + 1, local_sum, result)
    score_rows = jnp.broadcast_to(score_ref[...], (LANES, hidden_width))
    item_iota = lax.broadcasted_iota(jnp.int32, (n, item_rows), 1).astype(F32)
    group = max(1, 256 // n)
    for start in range(0, cap, group):
        ranks = range(start, min(start + group, cap))
        picks = []
        for r in ranks:
            index = recv1[:, 0, width + hidden_width + r : width + hidden_width + r + 1]
            picks.append((item_iota == index).astype(F32).astype(BF16))
        rows = dot(jnp.concatenate(picks, axis=0), table[...], NN)
        item_part = dot(rows.astype(BF16), first[feature_width:, :], NN)
        context = recv1[:, 0, width : width + hidden_width]
        hidden = silu(item_part + jnp.concatenate([context] * len(ranks), axis=0)).astype(BF16)
        second = silu(dot(hidden, second_w[...], NN)).astype(BF16)
        score = dot(second, score_rows, NT)
        for place, r in enumerate(ranks):
            mine = slice(place * n, (place + 1) * n)
            gen = jnp.sum(rows[mine] * queries, axis=1, keepdims=True)
            result = jnp.where(lane == r, score[mine], result)
            result = jnp.where(lane == gen_at + r, gen, result)
    send2[:, 0, :] = result

    exchange(send2, recv2, 1)
    sent(send1, 0)
    arrived(recv2, 1)

    back = recv2[:, 0, :]
    top = back.astype(BF16)
    rest = back - top.astype(F32)
    middle = rest.astype(BF16)
    bottom = (rest - middle.astype(F32)).astype(BF16)
    pieces = jnp.concatenate([top.astype(F32), middle.astype(F32), bottom.astype(F32)], axis=0)
    held_bf = held.astype(BF16)
    spread = dot(
        pieces.astype(BF16).T, jnp.concatenate([held_bf, held_bf, held_bf], axis=0), NN
    )
    score = jnp.sum(at_rank[:gen_at] * spread[:gen_at], axis=0, keepdims=True)
    gen = jnp.sum(at_rank[:gen_at] * spread[gen_at : 2 * gen_at], axis=0, keepdims=True)

    maxima = back[:, max_at : max_at + 1]
    sums = back[:, max_at + 1 : max_at + 2]
    peak = jnp.max(maxima, axis=0, keepdims=True)
    log_norm = peak + jnp.log(jnp.sum(sums * jnp.exp(maxima - peak), axis=0, keepdims=True))

    length = length_ref[0]
    position = lax.broadcasted_iota(jnp.int32, (1, slots), 1)
    live = position < length
    masked = jnp.where(live, score, -1e30)
    rank_peak = jnp.max(masked, axis=1, keepdims=True)
    rank_norm = rank_peak + jnp.log(
        jnp.sum(jnp.where(live, jnp.exp(masked - rank_peak), 0.0), axis=1, keepdims=True)
    )
    section = jnp.where(
        live, score - rank_norm + gen - log_norm + math.log(item_rows * n), 0.0
    )
    chosen = jnp.sum(jnp.where(position == slot_ref[0], section, 0.0), axis=1, keepdims=True)
    length_row = jnp.broadcast_to(length, (1, LANES)).astype(F32)
    prop_row = jnp.broadcast_to(prop_ref[0], (1, LANES)).astype(F32) / 1024.0
    section_ref[...] = section
    weight_ref[...] = chosen + (jnp.log(length_row) - jnp.log(prop_row))[:, :1]
    sent(send2, 1)


def solution(mesh):
    dp_size, item_size = mesh.shape["dp"], mesh.shape["item"]
    n = dp_size * item_size

    def body(
        query,
        item_table,
        context_features,
        candidates,
        lengths,
        logged_slot,
        logging_prop,
        w_first,
        w_second,
        w_score,
    ):
        slots = candidates.shape[1]
        cap = max(2, 3 * slots // (2 * n))
        width = query.shape[1]
        hidden_width = w_first.shape[1]
        message = width + hidden_width + LANES
        vmem = pl.BlockSpec(memory_space=pltpu.VMEM)
        smem = pl.BlockSpec(memory_space=pltpu.SMEM)
        hbm = pl.BlockSpec(memory_space=pl.ANY)
        section, weight = pl.pallas_call(
            functools.partial(kernel, dp_size, item_size, cap),
            out_shape=(
                jax.ShapeDtypeStruct((1, slots), F32),
                jax.ShapeDtypeStruct((1, 1), F32),
            ),
            in_specs=[vmem, vmem, vmem, smem, smem, smem, hbm, hbm, hbm, vmem],
            out_specs=(vmem, vmem),
            scratch_shapes=[
                pltpu.VMEM(item_table.shape, BF16),
                pltpu.VMEM(w_first.shape, BF16),
                pltpu.VMEM(w_second.shape, BF16),
                pltpu.VMEM((n, 1, message), F32),
                pltpu.VMEM((n, 1, message), F32),
                pltpu.VMEM((n, 1, LANES), F32),
                pltpu.VMEM((n, 1, LANES), F32),
                pltpu.SemaphoreType.DMA((3,)),
                pltpu.SemaphoreType.DMA((2,)),
                pltpu.SemaphoreType.DMA((2,)),
                pltpu.SemaphoreType.DMA((2,)),
            ],
            compiler_params=pltpu.CompilerParams(collective_id=0, has_side_effects=True),
            name="propensity",
        )(
            query,
            context_features,
            candidates,
            lengths,
            logged_slot,
            logging_prop,
            item_table,
            w_first,
            w_second,
            w_score.reshape(1, -1),
        )
        return section, weight.reshape(-1)

    split = P(("dp", "item"))
    rows = P(("dp", "item"), None)
    return jax.shard_map(
        body,
        mesh=mesh,
        in_specs=(rows, rows, rows, rows, split, split, split, P(), P(), P()),
        out_specs=(rows, split),
        check_vma=False,
    )
```

time: 185 us -> 30.4 us (0.16)
  blocking collectives: 112 us -> 0 us
  Pallas kernels: 0 us -> 24 us
  local copies, waits for them, and re-layouts: 18.2 us -> 1.86 us
  waiting for transfers between devices: 15.6 us -> 0 us
  starting transfers between devices: 15.4 us -> 0 us
  other arithmetic: 9.64 us -> 0 us
  matrix products: 7.17 us -> 0 us
    all_gather x1 -> x0, blocking collectives: 66.8 us -> none  [body(): gathered = lax.all_gather(query, ('dp', 'item'), axis=0, tiled=True)]
    unnamed x1 -> x0, blocking collectives: 37 us -> none
    pallas_call x0 -> x1, Pallas kernels: none -> 24 us  [body(): pl.pallas_call(functools.partial(kernel, dp_size, item_size, cap), out_sh...]
    all_to_all x3 -> x0, waiting for transfers between devices: 15.6 us -> none  [the longest x1 15.6 us: body(): lax.all_to_all(lax.all_to_all(item_table[local_index], 'dp', split_axis=0...]
    all_to_all x3 -> x0, starting transfers between devices: 15.4 us -> none  [the longest x1 6.09 us: body(): lax.all_to_all(lax.all_to_all(item_table[local_index], 'dp', split_axis=0...]
    gather x2 -> x0, local copies, waits for them, and re-layouts: 9.79 us -> none  [the longest x1 5.85 us: body(): item_table[local_index]]
    all_to_all x1 -> x0, blocking collectives: 7.87 us -> none  [body(): lax.all_to_all(outgoing, 'dp', split_axis=0, concat_axis=0, tiled=True)]
    dot_general x8 -> x0, matrix products: 7.17 us -> none  [the longest x4 4.97 us: sweep(): lax.dot_general(gathered, slab_rows, (((1,), (1,)), ((), ())), preferred_...]
  transfers between devices with their start and end apart: 3 -> 0, of which waited for: 1 -> 0; matrix products, arithmetic and copies ran while one was open for 4% -> 0% of each run, Pallas kernels for 0% -> 0%
where the time goes in v1:
time: 30.4 us; the launch traced here: 30.2 us
  Pallas kernels  24 us (79%)
  between operations  4.34 us (14%)
  local copies, waits for them, and re-layouts  1.86 us (6%)
    pallas_call x1, Pallas kernels, body(): pl.pallas_call(functools.partial(kernel, dp_size, item_size, cap), out_sh...  24 us
    unnamed x5, local copies, waits for them, and re-layouts  1.28 us

profile of v1, /device:TPU:0, one launch (start us, length us, event | category | flops | bytes accessed | tf_op | source)
XLA Modules:
  0.0 30.2 jit_solution(694757818884131639)
XLA Ops:
  1.9 0.0 copy-start.1
  2.6 0.0 copy-done.1
  2.6 0.6 %reshape.10.score_ref = bf16[1,512]{1,0:T(2,128)(2,1)} reshape(bf16[512]{0:T(512)(128)(2,1)S(1)} %copy-done.1) | data formatting | bytes 2048 | tf_op jit(solution)/shard_map/reshape | solution.py:291
  3.2 24.0 %propensity.1 = (f32[1,1024]{1,0:T(1,128)}, f32[1,1]{1,0:T(1,128)}) custom-call(bf16[1,256]{1,0:T(2,128)(2,1)} %query_ref.1, bf16[1,512]{1,0:T(2,128)(2,1)} %feature_ref.1, s32[1,1024]{1,0:T(1,128)} %cand_ref.1, s32[1]{0:T(128)S(6)} %copy.14.length_ref, s32[1]{0:T(128)S(6)} %copy.15.slot_ref, s32[1]{0:T(128)S(6)} %copy.16.prop_ref, ...), custom_call_target="tpu_custom_call" | custom-call | tf_op jit(solution)/shard_map/propensity/pallas_call | solution.py:258
  27.1 0.0 copy-start
  27.2 0.7 %copy-done = f32[1,1024]{1,0:T(1,128)S(1)} copy-done((f32[1,1024]{1,0:T(1,128)S(1)}, f32[1,1024]{1,0:T(1,128)}, u32[]{:S(2)}) %copy-start) | copy-done | bytes 4120
  27.8 0.6 %copy.17 = f32[1,1024]{1,0:T(1,128)} copy(f32[1,1024]{1,0:T(1,128)S(1)} %copy-done) | data formatting | bytes 8192
Async XLA Ops:
  1.9 0.7 %copy-start.1 = (bf16[512]{0:T(512)(128)(2,1)S(1)}, bf16[512]{0:T(512)(128)(2,1)}, u32[]{:S(2)}) copy-start(bf16[512]{0:T(512)(128)(2,1)} %param.19) | copy-start | bytes 3076
  27.1 0.7 %copy-start = (f32[1,1024]{1,0:T(1,128)S(1)}, f32[1,1024]{1,0:T(1,128)}, u32[]{:S(2)}) copy-start(f32[1,1024]{1,0:T(1,128)} %get-tuple-element.8) | copy-start | bytes 12292

commit v2 on v1

--- a/solution.py
+++ b/solution.py
@@ -32,19 +32,27 @@
 def kernel(
     dp_size,
     item_size,
+    groups,
     cap,
+    query_hbm,
+    feature_hbm,
+    cand_hbm,
+    length_hbm,
+    slot_hbm,
+    prop_hbm,
+    table_hbm,
+    first_hbm,
+    second_hbm,
+    score_hbm,
+    section_ref,
+    weight_ref,
     query_ref,
     feature_ref,
     cand_ref,
     length_ref,
     slot_ref,
     prop_ref,
-    table_hbm,
-    first_hbm,
-    second_hbm,
     score_ref,
-    section_ref,
-    weight_ref,
     table,
     first,
     second_w,
@@ -54,7 +62,8 @@
     recv2,
     load_sem,
     send_sem,
-    recv_sem,
+    arrive_sem,
+    return_sem,
     own_sem,
 ):
     n = dp_size * item_size
@@ -64,26 +73,54 @@
     hidden_width = first.shape[1]
     gen_at = round_up(cap, 8)
     max_at = 2 * gen_at
-    me = lax.axis_index("dp") * item_size + lax.axis_index("item")
+    dp_me, item_me = lax.axis_index("dp"), lax.axis_index("item")
+    me = dp_me * item_size + item_me
+    run = item_size // groups
+    members = dp_size * run
+    run_me = lax.div(item_me, run)
+    member_me = dp_me * run + lax.rem(item_me, run)
+
+    def device(offset, member):
+        dp = lax.div(member, run)
+        item = lax.rem(run_me + offset, groups) * run + lax.rem(member, run)
+        return dp * item_size + item, {"dp": dp, "item": item}
+
+    def each_peer(offset, act):
+        @pl.loop(1 if offset == 0 else 0, members)
+        def visit(j):
+            member = lax.rem(member_me + j, members)
+            peer, where = device(offset, member)
+            act(member, peer, where)
+
+    barrier = pltpu.get_barrier_semaphore()
+
+    def greet(member, peer, where):
+        pl.semaphore_signal(barrier, inc=1, device_id=where, device_id_type=pl.DeviceIdType.MESH)
+
+    far_first = sorted(range(groups), key=lambda g: -min(g, groups - g))
+    for offset in far_first:
+        each_peer(offset, greet)
 
     loads = [
-        pltpu.make_async_copy(first_hbm, first, load_sem.at[0]),
-        pltpu.make_async_copy(table_hbm, table, load_sem.at[1]),
-        pltpu.make_async_copy(second_hbm, second_w, load_sem.at[2]),
+        pltpu.make_async_copy(source, target, load_sem.at[i])
+        for i, (source, target) in enumerate(
+            [
+                (cand_hbm, cand_ref),
+                (query_hbm, query_ref),
+                (feature_hbm, feature_ref),
+                (first_hbm, first),
+                (table_hbm, table),
+                (second_hbm, second_w),
+                (score_hbm, score_ref),
+                (length_hbm, length_ref),
+                (slot_hbm, slot_ref),
+                (prop_hbm, prop_ref),
+            ]
+        )
     ]
     for load in loads:
         load.start()
-
-    def device(j):
-        peer = lax.rem(me + j, n)
-        return peer, {"dp": lax.div(peer, item_size), "item": lax.rem(peer, item_size)}
-
-    barrier = pltpu.get_barrier_semaphore()
-
-    @pl.loop(1, n)
-    def greet(j):
-        peer, where = device(j)
-        pl.semaphore_signal(barrier, inc=1, device_id=where, device_id_type=pl.DeviceIdType.MESH)
+    loads[0].wait()
 
     ids = cand_ref[...]
     holder = lax.div(ids, item_rows)
@@ -118,7 +155,8 @@
     asked = dot(parts, at_rank.astype(BF16), NT)
     asked = asked[:n] * float(LANES) + asked[n:]
 
-    loads[0].wait()
+    for load in loads[1:4]:
+        load.wait()
     context_part = dot(feature_ref[...], first[:feature_width, :], NN)
     send1[:, 0, :width] = jnp.broadcast_to(query_ref[...].astype(F32), (n, width))
     send1[:, 0, width : width + hidden_width] = jnp.broadcast_to(context_part, (n, hidden_width))
@@ -126,73 +164,115 @@
 
     pl.semaphore_wait(barrier, n - 1)
 
-    def exchange(source, target, index):
-        @pl.loop(1, n)
-        def send(j):
-            peer, where = device(j)
+    def ask(offset):
+        seen = (groups - offset) % groups
+
+        def act(member, peer, where):
             pltpu.make_async_remote_copy(
-                src_ref=source.at[pl.ds(peer, 1)],
-                dst_ref=target.at[pl.ds(me, 1)],
-                send_sem=send_sem.at[index],
-                recv_sem=recv_sem.at[index],
+                src_ref=send1.at[pl.ds(peer, 1)],
+                dst_ref=recv1.at[pl.ds(seen * members + member_me, 1)],
+                send_sem=send_sem.at[0],
+                recv_sem=arrive_sem.at[seen],
                 device_id=where,
                 device_id_type=pl.DeviceIdType.MESH,
             ).start()
 
-        own = pltpu.make_async_copy(
-            source.at[pl.ds(me, 1)], target.at[pl.ds(me, 1)], own_sem.at[index]
-        )
-        own.start()
-        own.wait()
-
-    def arrived(target, index):
-        pltpu.make_async_copy(
-            target.at[pl.ds(0, n - 1)], target.at[pl.ds(0, n - 1)], recv_sem.at[index]
-        ).wait()
-
-    def sent(source, index):
-        pltpu.make_async_copy(
-            source.at[pl.ds(0, n - 1)], source.at[pl.ds(0, n - 1)], send_sem.at[index]
-        ).wait()
-
-    exchange(send1, recv1, 0)
-    loads[1].wait()
-    loads[2].wait()
-    arrived(recv1, 0)
-
-    queries = recv1[:, 0, :width]
-    logits = dot(queries.astype(BF16), table[...], NT)
-    local_max = jnp.max(logits, axis=1, keepdims=True)
-    local_sum = jnp.sum(jnp.exp(logits - local_max), axis=1, keepdims=True)
-
-    lane = lax.broadcasted_iota(jnp.int32, (n, LANES), 1)
-    result = jnp.where(lane == max_at, local_max, 0.0)
-    result = jnp.where(lane == max_at + 1, local_sum, result)
-    score_rows = jnp.broadcast_to(score_ref[...], (LANES, hidden_width))
-    item_iota = lax.broadcasted_iota(jnp.int32, (n, item_rows), 1).astype(F32)
-    group = max(1, 256 // n)
-    for start in range(0, cap, group):
-        ranks = range(start, min(start + group, cap))
-        picks = []
-        for r in ranks:
-            index = recv1[:, 0, width + hidden_width + r : width + hidden_width + r + 1]
-            picks.append((item_iota == index).astype(F32).astype(BF16))
-        rows = dot(jnp.concatenate(picks, axis=0), table[...], NN)
+        each_peer(offset, act)
+
+    def give_back(offset):
+        def act(member, peer, where):
+            pltpu.make_async_remote_copy(
+                src_ref=send2.at[pl.ds(offset * members + member, 1)],
+                dst_ref=recv2.at[pl.ds(me, 1)],
+                send_sem=send_sem.at[1],
+                recv_sem=return_sem,
+                device_id=where,
+                device_id_type=pl.DeviceIdType.MESH,
+            ).start()
+
+        each_peer(offset, act)
+
+    def wait_rows(buffer, count, semaphore):
+        rows = buffer.at[pl.ds(0, count)]
+        pltpu.make_async_copy(rows, rows, semaphore).wait()
+
+    own_ask = pltpu.make_async_copy(
+        send1.at[pl.ds(me, 1)], recv1.at[pl.ds(member_me, 1)], own_sem.at[0]
+    )
+    own_ask.start()
+    for offset in far_first:
+        ask(offset)
+    for load in loads[4:]:
+        load.wait()
+    own_ask.wait()
+
+    lane = lax.broadcasted_iota(jnp.int32, (members, LANES), 1)
+    score_rows = jnp.broadcast_to(score_ref[...].reshape(1, hidden_width), (LANES, hidden_width))
+    item_iota = lax.broadcasted_iota(jnp.int32, (members, item_rows), 1).astype(F32)
+
+    def rank_group(group):
+        rows_here = pl.ds(group * members, members)
+        query = recv1[rows_here, 0, :width]
+        context = recv1[rows_here, 0, width : width + hidden_width]
+        wanted = recv1[rows_here, 0, width + hidden_width :]
+        picks = [
+            (item_iota == wanted[:, r : r + 1]).astype(F32) for r in range(cap)
+        ]
+        rows = dot(jnp.concatenate(picks, axis=0).astype(BF16), table[...], NN)
         item_part = dot(rows.astype(BF16), first[feature_width:, :], NN)
-        context = recv1[:, 0, width : width + hidden_width]
-        hidden = silu(item_part + jnp.concatenate([context] * len(ranks), axis=0)).astype(BF16)
+        hidden = silu(item_part + jnp.concatenate([context] * cap, axis=0)).astype(BF16)
         second = silu(dot(hidden, second_w[...], NN)).astype(BF16)
         score = dot(second, score_rows, NT)
-        for place, r in enumerate(ranks):
-            mine = slice(place * n, (place + 1) * n)
-            gen = jnp.sum(rows[mine] * queries, axis=1, keepdims=True)
+        result = jnp.zeros((members, LANES), F32)
+        for r in range(cap):
+            mine = slice(r * members, (r + 1) * members)
+            gen = jnp.sum(rows[mine] * query, axis=1, keepdims=True)
             result = jnp.where(lane == r, score[mine], result)
             result = jnp.where(lane == gen_at + r, gen, result)
-    send2[:, 0, :] = result
-
-    exchange(send2, recv2, 1)
-    sent(send1, 0)
-    arrived(recv2, 1)
+        return result
+
+    def normalizers():
+        logits = dot(recv1[:, 0, :width].astype(BF16), table[...], NT)
+        local_max = jnp.max(logits, axis=1, keepdims=True)
+        local_sum = jnp.sum(jnp.exp(logits - local_max), axis=1, keepdims=True)
+        return local_max, local_sum
+
+    order = sorted(range(groups), key=lambda g: min(g, groups - g))
+    order = order[:-2] + order[:-3:-1]
+    results = {}
+    waited = set()
+
+    def wait_group(group):
+        if group not in waited:
+            waited.add(group)
+            wait_rows(recv1, members - 1 if group == 0 else members, arrive_sem.at[group])
+
+    for group in order[:-2]:
+        wait_group(group)
+        results[group] = rank_group(group)
+    for group in order[-2:]:
+        wait_group(group)
+    local_max, local_sum = normalizers()
+
+    def finish(group):
+        mine = slice(group * members, (group + 1) * members)
+        result = jnp.where(lane == max_at, local_max[mine], results[group])
+        result = jnp.where(lane == max_at + 1, local_sum[mine], result)
+        send2[pl.ds(group * members, members), 0, :] = result
+        give_back(group)
+
+    for group in reversed(order[:-2]):
+        finish(group)
+    own_back = pltpu.make_async_copy(
+        send2.at[pl.ds(member_me, 1)], recv2.at[pl.ds(me, 1)], own_sem.at[1]
+    )
+    own_back.start()
+    for group in order[-2:]:
+        results[group] = rank_group(group)
+        finish(group)
+    own_back.wait()
+    wait_rows(send1, n - 1, send_sem.at[0])
+    wait_rows(recv2, n - 1, return_sem)
 
     back = recv2[:, 0, :]
     top = back.astype(BF16)
@@ -228,7 +308,7 @@
     prop_row = jnp.broadcast_to(prop_ref[0], (1, LANES)).astype(F32) / 1024.0
     section_ref[...] = section
     weight_ref[...] = chosen + (jnp.log(length_row) - jnp.log(prop_row))[:, :1]
-    sent(send2, 1)
+    wait_rows(send2, n - 1, send_sem.at[1])
 
 
 def solution(mesh):
@@ -253,17 +333,24 @@
         hidden_width = w_first.shape[1]
         message = width + hidden_width + LANES
         vmem = pl.BlockSpec(memory_space=pltpu.VMEM)
-        smem = pl.BlockSpec(memory_space=pltpu.SMEM)
+        groups = math.gcd(4, item_size)
         hbm = pl.BlockSpec(memory_space=pl.ANY)
         section, weight = pl.pallas_call(
-            functools.partial(kernel, dp_size, item_size, cap),
+            functools.partial(kernel, dp_size, item_size, groups, cap),
             out_shape=(
-                jax.ShapeDtypeStruct((1, slots), F32),
-                jax.ShapeDtypeStruct((1, 1), F32),
+                pltpu.VMEM((1, slots), F32),
+                pltpu.VMEM((1, 1), F32),
             ),
-            in_specs=[vmem, vmem, vmem, smem, smem, smem, hbm, hbm, hbm, vmem],
+            in_specs=[pl.BlockSpec(memory_space=pltpu.HBM)] * 10,
             out_specs=(vmem, vmem),
             scratch_shapes=[
+                pltpu.VMEM(query.shape, BF16),
+                pltpu.VMEM(context_features.shape, BF16),
+                pltpu.VMEM(candidates.shape, jnp.int32),
+                pltpu.SMEM(lengths.shape, jnp.int32),
+                pltpu.SMEM(logged_slot.shape, jnp.int32),
+                pltpu.SMEM(logging_prop.shape, jnp.int32),
+                pltpu.VMEM(w_score.shape, BF16),
                 pltpu.VMEM(item_table.shape, BF16),
                 pltpu.VMEM(w_first.shape, BF16),
                 pltpu.VMEM(w_second.shape, BF16),
@@ -271,9 +358,10 @@
                 pltpu.VMEM((n, 1, message), F32),
                 pltpu.VMEM((n, 1, LANES), F32),
                 pltpu.VMEM((n, 1, LANES), F32),
-                pltpu.SemaphoreType.DMA((3,)),
+                pltpu.SemaphoreType.DMA((10,)),
                 pltpu.SemaphoreType.DMA((2,)),
-                pltpu.SemaphoreType.DMA((2,)),
+                pltpu.SemaphoreType.DMA((groups,)),
+                pltpu.SemaphoreType.DMA,
                 pltpu.SemaphoreType.DMA((2,)),
             ],
             compiler_params=pltpu.CompilerParams(collective_id=0, has_side_effects=True),
@@ -288,7 +376,7 @@
             item_table,
             w_first,
             w_second,
-            w_score.reshape(1, -1),
+            w_score,
         )
         return section, weight.reshape(-1)
 

time: 30.4 us -> 28.7 us (0.944)
  local copies, waits for them, and re-layouts: 1.86 us -> 0.6 us
  between operations: 4.34 us -> 3.74 us
    unnamed x5 -> x1, local copies, waits for them, and re-layouts: 1.28 us -> 0.6 us
    reshape x1 -> x0, local copies, waits for them, and re-layouts: 0.58 us -> none  [body(): w_score.reshape(1, -1)]
where the time goes in v2:
time: 28.7 us; the launch traced here: 28.5 us
  Pallas kernels  24.2 us (84%)
  between operations  3.74 us (13%)
  local copies, waits for them, and re-layouts  0.6 us (2%)
    pallas_call x1, Pallas kernels, body(): pl.pallas_call(functools.partial(kernel, dp_size, item_size, groups, cap)...  24.2 us
    unnamed x1, local copies, waits for them, and re-layouts  0.6 us

profile of v2, /device:TPU:0, one launch (start us, length us, event | category | flops | bytes accessed | tf_op | source)
XLA Modules:
  0.0 28.5 jit_solution(5676446855692876237)
XLA Ops:
  2.6 24.2 %propensity.1 = (f32[1,1024]{1,0:T(1,128)S(1)}, f32[1,1]{1,0:T(1,128)S(1)}) custom-call(bf16[1,256]{1,0:T(2,128)(2,1)} %query_hbm.1, bf16[1,512]{1,0:T(2,128)(2,1)} %feature_hbm.1, s32[1,1024]{1,0:T(1,128)} %cand_hbm.1, s32[1]{0:T(128)S(6)} %copy.16.length_hbm, s32[1]{0:T(128)S(6)} %copy.17.slot_hbm, s32[1]{0:T(128)S(6)} %copy.18.prop_hbm, ...), custom_call_target="tpu_custom_call" | custom-call | tf_op jit(solution)/shard_map/propensity/pallas_call | solution.py:338
  26.8 0.6 %copy.14 = f32[1,1024]{1,0:T(1,128)} copy(f32[1,1024]{1,0:T(1,128)S(1)} %get-tuple-element.6) | data formatting | bytes 8192

commit v3 on v2

--- a/solution.py
+++ b/solution.py
@@ -37,9 +37,7 @@
     query_hbm,
     feature_hbm,
     cand_hbm,
-    length_hbm,
-    slot_hbm,
-    prop_hbm,
+    scalar_hbm,
     table_hbm,
     first_hbm,
     second_hbm,
@@ -49,9 +47,7 @@
     query_ref,
     feature_ref,
     cand_ref,
-    length_ref,
-    slot_ref,
-    prop_ref,
+    scalar_ref,
     score_ref,
     table,
     first,
@@ -65,6 +61,11 @@
     arrive_sem,
     return_sem,
     own_sem,
+    items,
+    found,
+    wanted_v,
+    wanted_at,
+    index_sem,
 ):
     n = dp_size * item_size
     item_rows, width = table.shape
@@ -112,9 +113,7 @@
                 (table_hbm, table),
                 (second_hbm, second_w),
                 (score_hbm, score_ref),
-                (length_hbm, length_ref),
-                (slot_hbm, slot_ref),
-                (prop_hbm, prop_ref),
+                (scalar_hbm, scalar_ref),
             ]
         )
     ]
@@ -208,18 +207,46 @@
 
     lane = lax.broadcasted_iota(jnp.int32, (members, LANES), 1)
     score_rows = jnp.broadcast_to(score_ref[...].reshape(1, hidden_width), (LANES, hidden_width))
-    item_iota = lax.broadcasted_iota(jnp.int32, (members, item_rows), 1).astype(F32)
+    hidden_tiles = hidden_width // LANES
+    tall = items.shape[1]
+    step = math.gcd(256, item_rows)
+
+    @pl.loop(0, item_rows // step)
+    def project(i):
+        part = pl.ds(pl.multiple_of(i * step, step), step)
+        block = table[part]
+        projected = dot(block, first[feature_width:, :], NN)
+        for j in range(hidden_tiles):
+            items[part, j] = projected[:, j * LANES : (j + 1) * LANES]
+        for j in range(width // LANES):
+            items[part, hidden_tiles + j] = block[:, j * LANES : (j + 1) * LANES].astype(F32)
+
+
+    def to_scalar(group):
+        rows_here = pl.ds(group * members, members)
+        return pltpu.make_async_copy(
+            wanted_v.at[rows_here], wanted_at.at[rows_here], index_sem.at[group]
+        )
 
     def rank_group(group):
         rows_here = pl.ds(group * members, members)
         query = recv1[rows_here, 0, :width]
         context = recv1[rows_here, 0, width : width + hidden_width]
-        wanted = recv1[rows_here, 0, width + hidden_width :]
-        picks = [
-            (item_iota == wanted[:, r : r + 1]).astype(F32) for r in range(cap)
-        ]
-        rows = dot(jnp.concatenate(picks, axis=0).astype(BF16), table[...], NN)
-        item_part = dot(rows.astype(BF16), first[feature_width:, :], NN)
+        to_scalar(group).wait()
+        for r in range(cap):
+            for c in range(members):
+                at = jnp.clip(wanted_at[group * members + c, 0, r], 0, item_rows - 1)
+                place = (group * cap + r) * members + c
+                found[pl.ds(place * tall, tall)] = items[at]
+        count = cap * members
+
+        def found_tile(j):
+            return found[pl.ds(group * count * tall + j, count, stride=tall), :]
+
+        item_part = jnp.concatenate([found_tile(j) for j in range(hidden_tiles)], axis=1)
+        rows = jnp.concatenate(
+            [found_tile(hidden_tiles + j) for j in range(width // LANES)], axis=1
+        )
         hidden = silu(item_part + jnp.concatenate([context] * cap, axis=0)).astype(BF16)
         second = silu(dot(hidden, second_w[...], NN)).astype(BF16)
         score = dot(second, score_rows, NT)
@@ -246,6 +273,9 @@
         if group not in waited:
             waited.add(group)
             wait_rows(recv1, members - 1 if group == 0 else members, arrive_sem.at[group])
+            rows_here = pl.ds(group * members, members)
+            wanted_v[rows_here] = recv1[rows_here, :, width + hidden_width :].astype(jnp.int32)
+            to_scalar(group).start()
 
     for group in order[:-2]:
         wait_group(group)
@@ -292,7 +322,7 @@
     peak = jnp.max(maxima, axis=0, keepdims=True)
     log_norm = peak + jnp.log(jnp.sum(sums * jnp.exp(maxima - peak), axis=0, keepdims=True))
 
-    length = length_ref[0]
+    length = scalar_ref[:, 0:1]
     position = lax.broadcasted_iota(jnp.int32, (1, slots), 1)
     live = position < length
     masked = jnp.where(live, score, -1e30)
@@ -303,11 +333,10 @@
     section = jnp.where(
         live, score - rank_norm + gen - log_norm + math.log(item_rows * n), 0.0
     )
-    chosen = jnp.sum(jnp.where(position == slot_ref[0], section, 0.0), axis=1, keepdims=True)
-    length_row = jnp.broadcast_to(length, (1, LANES)).astype(F32)
-    prop_row = jnp.broadcast_to(prop_ref[0], (1, LANES)).astype(F32) / 1024.0
+    chosen = jnp.sum(jnp.where(position == scalar_ref[:, 1:2], section, 0.0), axis=1, keepdims=True)
+    prop = scalar_ref[:, 2:3].astype(F32) / 1024.0
     section_ref[...] = section
-    weight_ref[...] = chosen + (jnp.log(length_row) - jnp.log(prop_row))[:, :1]
+    weight_ref[...] = chosen + jnp.log(length.astype(F32)) - jnp.log(prop)
     wait_rows(send2, n - 1, send_sem.at[1])
 
 
@@ -332,24 +361,24 @@
         width = query.shape[1]
         hidden_width = w_first.shape[1]
         message = width + hidden_width + LANES
+        tall = round_up((width + hidden_width) // LANES, 8)
         vmem = pl.BlockSpec(memory_space=pltpu.VMEM)
         groups = math.gcd(4, item_size)
-        hbm = pl.BlockSpec(memory_space=pl.ANY)
+        lane = lax.broadcasted_iota(jnp.int32, (1, LANES), 1)
+        scalars = jnp.where(lane == 0, lengths, jnp.where(lane == 1, logged_slot, logging_prop))
         section, weight = pl.pallas_call(
             functools.partial(kernel, dp_size, item_size, groups, cap),
             out_shape=(
                 pltpu.VMEM((1, slots), F32),
                 pltpu.VMEM((1, 1), F32),
             ),
-            in_specs=[pl.BlockSpec(memory_space=pltpu.HBM)] * 10,
+            in_specs=[pl.BlockSpec(memory_space=pltpu.HBM)] * 8,
             out_specs=(vmem, vmem),
             scratch_shapes=[
                 pltpu.VMEM(query.shape, BF16),
                 pltpu.VMEM(context_features.shape, BF16),
                 pltpu.VMEM(candidates.shape, jnp.int32),
-                pltpu.SMEM(lengths.shape, jnp.int32),
-                pltpu.SMEM(logged_slot.shape, jnp.int32),
-                pltpu.SMEM(logging_prop.shape, jnp.int32),
+                pltpu.VMEM((1, LANES), jnp.int32),
                 pltpu.VMEM(w_score.shape, BF16),
                 pltpu.VMEM(item_table.shape, BF16),
                 pltpu.VMEM(w_first.shape, BF16),
@@ -358,11 +387,16 @@
                 pltpu.VMEM((n, 1, message), F32),
                 pltpu.VMEM((n, 1, LANES), F32),
                 pltpu.VMEM((n, 1, LANES), F32),
-                pltpu.SemaphoreType.DMA((10,)),
+                pltpu.SemaphoreType.DMA((8,)),
                 pltpu.SemaphoreType.DMA((2,)),
                 pltpu.SemaphoreType.DMA((groups,)),
                 pltpu.SemaphoreType.DMA,
                 pltpu.SemaphoreType.DMA((2,)),
+                pltpu.VMEM((item_table.shape[0], tall, LANES), F32),
+                pltpu.VMEM((n * cap * tall + tall, LANES), F32),
+                pltpu.VMEM((n, 1, LANES), jnp.int32),
+                pltpu.SMEM((n, 1, LANES), jnp.int32),
+                pltpu.SemaphoreType.DMA((groups,)),
             ],
             compiler_params=pltpu.CompilerParams(collective_id=0, has_side_effects=True),
             name="propensity",
@@ -370,9 +404,7 @@
             query,
             context_features,
             candidates,
-            lengths,
-            logged_slot,
-            logging_prop,
+            scalars,
             item_table,
             w_first,
             w_second,

time: 28.7 us -> 26.8 us (0.934)
  Pallas kernels: 24.2 us -> 21.7 us
  other arithmetic: 0 us -> 0.54 us
    pallas_call x1, Pallas kernels: 24.2 us -> 21.7 us  [body(): pl.pallas_call(functools.partial(kernel, dp_size, item_size, groups, cap)...]
    select_n x0 -> x1, other arithmetic: none -> 0.54 us  [body(): jnp.where(lane == 0, lengths, jnp.where(lane == 1, logged_slot, logging_p...]
where the time goes in v3:
time: 26.8 us; the launch traced here: 26.6 us
  Pallas kernels  21.7 us (81%)
  between operations  3.74 us (14%)
  local copies, waits for them, and re-layouts  0.6 us (2%)
  other arithmetic  0.54 us (2%)
    pallas_call x1, Pallas kernels, body(): pl.pallas_call(functools.partial(kernel, dp_size, item_size, groups, cap)...  21.7 us
    unnamed x1, local copies, waits for them, and re-layouts  0.6 us
    select_n x1, other arithmetic, body(): jnp.where(lane == 0, lengths, jnp.where(lane == 1, logged_slot, logging_p...  0.54 us

profile of v3, /device:TPU:0, one launch (start us, length us, event | category | flops | bytes accessed | tf_op | source)
XLA Modules:
  0.0 26.6 jit_solution(17484200339713376313)
XLA Ops:
  2.6 0.5 %compare_select_fusion.1.scalar_hbm = s32[1,128]{1,0:T(1,128)} fusion(s32[]{:T(128)} %bitcast.6, s32[]{:T(128)} %bitcast.5, s32[]{:T(128)} %bitcast.4), kind=kLoop, calls=%fused_computation.1 | loop fusion | flops 512 | bytes 524 | tf_op jit(solution)/shard_map/jit(_where)/select_n | solution.py:368
  3.1 21.7 %propensity.1 = (f32[1,1024]{1,0:T(1,128)S(1)}, f32[1,1]{1,0:T(1,128)S(1)}) custom-call(bf16[1,256]{1,0:T(2,128)(2,1)} %query_hbm.1, bf16[1,512]{1,0:T(2,128)(2,1)} %feature_hbm.1, s32[1,1024]{1,0:T(1,128)} %cand_hbm.1, s32[1,128]{1,0:T(1,128)} %compare_select_fusion.1.scalar_hbm, bf16[2048,256]{1,0:T(8,128)(2,1)} %table_hbm.1, bf16[768,512]{1,0:T(8,128)(2,1)} %first_hbm.1, ...), custom_call_target="tpu_custom_call" | custom-call | tf_op jit(solution)/shard_map/propensity/pallas_call | solution.py:369
  24.9 0.6 %copy.14 = f32[1,1024]{1,0:T(1,128)} copy(f32[1,1024]{1,0:T(1,128)S(1)} %get-tuple-element.6) | data formatting | bytes 8192
